TPU v7x, 32 devices: a whole 2x2x4 slice. The times are simulated.
32 devices in a mesh: parts: 2 (over y), tensor: 4 (over z), dp: 4 (over x, core).
Axes of the slice: x: 2, y: 2, z: 4, core: 2. Of those that a mesh axis runs over, the one named last changes fastest.
Arguments:
- inputs: bfloat16 [4096, 8192], P(('parts', 'dp'), 'tensor'), parts along dimension 0, may hold values from -6 to 6
- cotangent: bfloat16 [4096, 8192], P(('parts', 'dp'), 'tensor'), parts along dimension 0, may hold values from -6 to 6
- weight: bfloat16 [8192, 8192], P(None, 'tensor'), may hold values from -0.0625 to 0.0625
- down_weight_maps: bfloat16 [8192, 2048], P('tensor', 'parts'), parts along dimension 1, may hold values from -0.0625 to 0.0625
- up_weight_maps: bfloat16 [2048, 8192], P('parts', 'tensor'), parts along dimension 0, may hold values from -0.75 to 0.75
- counts: int32 [8, 16], P('parts'), parts along dimension 0, may hold values from 0 to 256, as said below
- ranks: int32 [32], P('parts'), parts along dimension 0, may hold values from 8 to 64, as said below
- owners: int32 [32], P('parts'), parts along dimension 0, may hold values from 0 to 3
Outputs:
- projected: bfloat16 [4096, 8192], P(('parts', 'dp'), 'tensor'), parts along dimension 0
- input_grad: bfloat16 [4096, 8192], P(('parts', 'dp'), 'tensor'), parts along dimension 0
- grad_a: float32 [8, 8192, 1024], P(('parts', 'dp'), 'tensor'), parts along dimension 0
- grad_b: float32 [8, 1024, 8192], P(('parts', 'dp'), None, 'tensor'), parts along dimension 0
There are 2 independent parts, one for each index of `parts`. A program takes and returns all parts, laid end to end along the dimension named above; an argument that names none is the same for every part. Nothing has to cross between parts.
Inputs may be any that keep to these rules, and one draw needn't show every extreme that they name: `counts`: each row sums to at most 512, one row to exactly 512, and all rows together to exactly 1024; some entry is exactly 256. `ranks`: each rank is 64 divided by 1, 2, 4 or 8; some trial has 64 and some 64 // 8.
All inputs are finite; a program needn't handle non-finite values.
Results may differ from a plain program's by a relative error of at most 0.0034.
Values may be sent and summed in bfloat16 or wider, within the bound.
A program may use at most 256 MiB of HBM per device.

v0:
```python
import jax
import jax.numpy as jnp
from jax import lax
from jax.sharding import PartitionSpec as P

LARGEST_RANK = 64
TRIALS = 16
LANES = 128
adapter_alpha = 16.0
TRAILING = (((1,), (1,)), ((), ()))
FIRST = (((0,), (0,)), ((), ()))


def fold_columns(values, match):
    width = values.shape[1]
    kept = jnp.where(match, values, 0.0)
    return sum((kept[:, i : i + LANES] for i in range(0, width, LANES)))


def spread_columns(folded, match):
    repeats = match.shape[1] // LANES
    return jnp.where(
        match, jnp.concatenate([folded] * repeats, axis=1), jnp.zeros((), folded.dtype)
    )


def local(inputs, cotangent, weight, down_weight_maps, up_weight_maps, counts, ranks, owners):
    slot_count, feature_local = inputs.shape
    group_count = counts.shape[0]
    width = down_weight_maps.shape[1]
    column = jnp.arange(width, dtype=jnp.int32)
    col_trial = column // LARGEST_RANK
    column_slot = column % LARGEST_RANK
    trial_ids = jnp.arange(TRIALS, dtype=jnp.int32)
    matches = col_trial[:, None] == trial_ids[None, :]
    rank_per_column = jnp.sum(jnp.where(matches, ranks[None, :], 0), axis=1)
    owner_col = jnp.sum(jnp.where(matches, owners[None, :], 0), axis=1)
    scale_per_column = jnp.where(
        column_slot < rank_per_column, adapter_alpha / rank_per_column.astype(jnp.float32), 0.0
    )
    trial_rows = jnp.sum(counts, axis=0)
    per_trial = 1.0 / jnp.maximum(trial_rows, 1).astype(jnp.float32)
    inverse_col = jnp.sum(jnp.where(matches, per_trial[None, :], 0.0), axis=1)
    cumulative = jnp.cumsum(counts, axis=1)
    group_ids = jnp.arange(group_count, dtype=jnp.int32)
    my_group = lax.axis_index("dp")
    positions = jnp.arange(slot_count, dtype=jnp.int32)
    trial_all = jnp.sum(
        (positions[None, :, None] >= cumulative[:, None, :]).astype(jnp.int32), axis=2
    )
    row_trial = jnp.sum(jnp.where((group_ids == my_group)[:, None], trial_all, 0), axis=0)
    is_live = row_trial < TRIALS
    match = row_trial[:, None] == col_trial[None, :]
    match_all = trial_all.reshape(-1)[:, None] == col_trial[None, :]
    coef = jnp.where(match, scale_per_column[None, :], 0.0)
    coef_folded = fold_columns(coef, match)
    down_part = jnp.dot(inputs, down_weight_maps, preferred_element_type=jnp.float32)
    back_part = lax.dot_general(
        cotangent, up_weight_maps, TRAILING, preferred_element_type=jnp.float32
    )
    folded = jnp.concatenate(
        [fold_columns(down_part, match), fold_columns(back_part, match)], axis=1
    )
    folded = lax.psum(folded, "tensor")
    scaled_down_f = (coef_folded * folded[:, :LANES]).astype(jnp.bfloat16)
    scaled_back_f = (coef_folded * folded[:, LANES:]).astype(jnp.bfloat16)
    all_inputs = lax.all_gather(inputs, "tensor", axis=1, tiled=True)
    mine = lax.axis_index("tensor")
    block = jnp.arange(weight.shape[0], dtype=jnp.int32) // feature_local
    frozen_back = lax.dot_general(cotangent, weight, TRAILING, preferred_element_type=jnp.float32)
    others = jnp.where((block == mine)[None, :], 0.0, frozen_back).astype(jnp.bfloat16)
    others_share = lax.psum_scatter(others, "tensor", scatter_dimension=1, tiled=True)
    own_weight = lax.dynamic_slice_in_dim(weight, mine * feature_local, feature_local, 0)
    own_share = lax.dot_general(cotangent, own_weight, TRAILING, preferred_element_type=jnp.float32)
    frozen_share = own_share + others_share.astype(jnp.float32)
    group_inputs = lax.all_gather(inputs, "dp", axis=0, tiled=True)
    group_cotangent = lax.all_gather(cotangent, "dp", axis=0, tiled=True)
    both = lax.all_gather(
        jnp.concatenate([scaled_down_f, scaled_back_f], axis=1), "dp", axis=0, tiled=True
    )
    frozen_output = jnp.dot(all_inputs, weight, preferred_element_type=jnp.float32)
    scaled_down = spread_columns(scaled_down_f, match)
    scaled_back = spread_columns(scaled_back_f, match)
    merged = frozen_output + jnp.dot(
        scaled_down, up_weight_maps, preferred_element_type=jnp.float32
    )
    projected = jnp.where(is_live[:, None], merged, 0.0).astype(jnp.bfloat16)
    adapter_in = lax.dot_general(
        scaled_back, down_weight_maps, TRAILING, preferred_element_type=jnp.float32
    )
    input_grad = jnp.where(is_live[:, None], frozen_share + adapter_in, 0.0).astype(jnp.bfloat16)
    owned = jnp.where(owner_col == my_group, inverse_col, 0.0)
    down_all = spread_columns(both[:, :LANES], match_all)
    back_all = spread_columns(both[:, LANES:], match_all)
    grad_a = lax.dot_general(group_inputs, back_all, FIRST, preferred_element_type=jnp.float32)
    grad_b = lax.dot_general(down_all, group_cotangent, FIRST, preferred_element_type=jnp.float32)
    grad_a = (grad_a * owned[None, :])[None]
    grad_b = (grad_b * owned[:, None])[None]
    return (projected, input_grad, grad_a, grad_b)


def solution(mesh):
    return jax.shard_map(
        local,
        mesh=mesh,
        in_specs=(
            P(("parts", "dp"), "tensor"),
            P(("parts", "dp"), "tensor"),
            P(None, "tensor"),
            P("tensor", "parts"),
            P("parts", "tensor"),
            P("parts", None),
            P("parts"),
            P("parts"),
        ),
        out_specs=(
            P(("parts", "dp"), "tensor"),
            P(("parts", "dp"), "tensor"),
            P(("parts", "dp"), "tensor", None),
            P(("parts", "dp"), None, "tensor"),
        ),
        check_vma=False,
    )
```

profile of v0, /device:TPU:0, one launch (start us, length us, event | category | flops | bytes accessed | tf_op | source)
XLA Modules:
  0.0 511.5 jit_solution(14548352022868119628)
XLA Ops:
  8.3 5.3 %compare_select_fusion.4 = f32[512,1024]{1,0:T(8,128)S(1)} fusion(bf16[512,2048]{1,0:T(8,128)(2,1)} %param.9, bf16[1024,2048]{1,0:T(8,128)(2,1)} %param.12, s32[1024]{0:T(1024)S(1)} %add_select_fusion.1, s32[512]{0:T(512)S(1)} %select_reduce_fusion.3), kind=kOutput, calls=%fused_computation.9 | convolution fusion | flops 2148532224 | bytes 8394752 | tf_op jit(solution)/shard_map/dot_general | solution.py:58
  13.8 2.3 compare_select_fusion.5
  17.6 40.7 %all-reduce.2.cloned.1.call-done = f32[512,256]{1,0:T(8,128)} async-done(((f32[512,256]{1,0:T(8,128)}), f32[512,256]{1,0:T(8,128)}) %all-reduce.2.cloned.1.call-update) | async-done | bytes 524304 | tf_op jit(solution)/shard_map/psum | solution.py:64
  58.2 1.1 constant_dynamic-update-slice_fusion.15
  59.3 1.8 constant_dynamic-update-slice_fusion.7
  64.0 24.4 %select_convert_fusion = bf16[512,8192]{1,0:T(8,128)(2,1)} fusion(bf16[512,2048]{1,0:T(8,128)(2,1)S(1)} %copy-done.2, bf16[8192,2048]{1,0:T(8,128)(2,1)} %param.10, pred[8192]{0:T(1024)(128)(4,1)S(1)} %fusion.23), kind=kOutput, calls=%fused_computation | convolution fusion | flops 17188257792 | bytes 44048384 | tf_op jit(solution)/shard_map/dot_general | solution.py:70
  89.6 7.7 %fusion.14 = f32[512,2048]{1,0:T(8,128)} fusion(bf16[2048,1024]{1,0:T(8,128)(2,1)} %param.11, bf16[512,1024]{1,0:T(8,128)(2,1)S(1)} %constant_dynamic-update-slice_fusion.8, s32[1024]{0:T(1024)S(1)} %add_select_fusion.1, s32[512]{0:T(512)S(1)} %select_reduce_fusion.3), kind=kOutput, calls=%fused_computation.25 | convolution fusion | flops 2148532224 | bytes 9443328 | tf_op jit(solution)/shard_map/dot_general | solution.py:88
  97.6 4.4 fusion.13
  102.0 2.0 slice_dynamic-update-slice_fusion.6
  104.0 2.0 slice_dynamic-update-slice_fusion.5
  106.0 1.9 slice_dynamic-update-slice_fusion.4
  107.9 1.9 slice_dynamic-update-slice_fusion.3
  110.6 0.9 slice_dynamic-update-slice_fusion.1
  111.5 0.9 slice_dynamic-update-slice_fusion
  112.4 1.0 slice_dynamic-update-slice_fusion.7
  119.2 19.4 %all-gather.9.cloned.1.call-done = bf16[2048,2048]{1,0:T(8,128)(2,1)} async-done(((bf16[512,2048]{1,0:T(8,128)(2,1)}), bf16[2048,2048]{1,0:T(8,128)(2,1)}) %all-gather.9.cloned.1.call-update) | async-done | bytes 8388624 | tf_op jit(solution)/shard_map/all_gather | solution.py:76
  138.6 14.9 %multiply_bitcast_fusion.1 = f32[1,2048,1024]{1,2,0:T(8,128)} fusion(bf16[2048,2048]{1,0:T(8,128)(2,1)} %all-gather.9.cloned.1.call-done, bf16[2048,1024]{1,0:T(8,128)(2,1)} %slice_dynamic-update-slice_fusion.15, f32[1024]{0:T(1024)S(1)} %compare_select_fusion.12, s32[1024]{0:T(1024)S(1)} %add_select_fusion.1, s32[2048]{0:T(1024)S(1)} %bitcast.30), kind=kOutput, calls=%fused_computation.4 | convolution fusion | flops 8596226048 | bytes 20987904 | tf_op jit(solution)/shard_map/dot_general | solution.py:95
  153.5 9.2 %copy.15 = f32[1,2048,1024]{2,1,0:T(8,128)} copy(f32[1,2048,1024]{1,2,0:T(8,128)} %multiply_bitcast_fusion.1) | data formatting | bytes 16777216
  162.7 35.6 %all-gather.11.cloned.1.call-done = bf16[2048,2048]{1,0:T(8,128)(2,1)} async-done(((bf16[512,2048]{1,0:T(8,128)(2,1)}), bf16[2048,2048]{1,0:T(8,128)(2,1)}) %all-gather.11.cloned.1.call-update) | async-done | bytes 8388624 | tf_op jit(solution)/shard_map/all_gather | solution.py:77
  198.3 14.9 %multiply_bitcast_fusion = f32[1,1024,2048]{2,1,0:T(8,128)} fusion(bf16[2048,2048]{1,0:T(8,128)(2,1)} %all-gather.11.cloned.1.call-done, bf16[2048,1024]{1,0:T(8,128)(2,1)} %get-tuple-element.19, f32[1024]{0:T(1024)S(1)} %compare_select_fusion.12, s32[1024]{0:T(1024)S(1)} %add_select_fusion.1, s32[2048]{0:T(1024)S(1)} %bitcast.31), kind=kOutput, calls=%fused_computation.3 | convolution fusion | flops 8596226048 | bytes 20987904 | tf_op jit(solution)/shard_map/dot_general | solution.py:96
  213.2 136.2 %all-gather.5.cloned.1.call-done = bf16[512,8192]{1,0:T(8,128)(2,1)} async-done(((bf16[512,2048]{1,0:T(8,128)(2,1)}), bf16[512,8192]{1,0:T(8,128)(2,1)}) %all-gather.5.cloned.1.call-update) | async-done | bytes 8388624 | tf_op jit(solution)/shard_map/all_gather | solution.py:67
  349.4 24.9 %select_convert_fusion.1 = bf16[512,2048]{1,0:T(8,128)(2,1)} fusion(f32[512,2048]{1,0:T(8,128)} %fusion.13, bf16[512,8192]{1,0:T(8,128)(2,1)} %all-gather.5.cloned.1.call-done, bf16[8192,2048]{1,0:T(8,128)(2,1)} %param.10, pred[512]{0:T(512)(128)(4,1)S(1)} %broadcast_compare_fusion), kind=kOutput, calls=%fused_computation.19 | convolution fusion | flops 17183014912 | bytes 48235008 | tf_op jit(solution)/shard_map/dot_general | solution.py:81
  374.3 120.0 %reduce-scatter.2.cloned.1.call-done = bf16[512,2048]{1,0:T(8,128)(2,1)} async-done(((bf16[512,8192]{1,0:T(8,128)(2,1)}), bf16[512,2048]{1,0:T(8,128)(2,1)}) %reduce-scatter.2.cloned.1.call-update) | async-done | bytes 2097168 | tf_op jit(solution)/shard_map/reduce_scatter | solution.py:72
  494.3 10.3 %fusion.4 = bf16[512,2048]{1,0:T(8,128)(2,1)} fusion(f32[512,2048]{1,0:T(8,128)} %fusion.14, bf16[512,2048]{1,0:T(8,128)(2,1)} %reduce-scatter.2.cloned.1.call-done, bf16[512,2048]{1,0:T(8,128)(2,1)S(1)} %copy-done.2, bf16[8192,2048]{1,0:T(8,128)(2,1)} %param.10, s32[]{:T(128)S(6)} %select_n.128, pred[512]{0:T(512)(128)(4,1)S(1)} %broadcast_compare_fusion), kind=kOutput, calls=%fused_computation.16 | convolution fusion | flops 4300210176 | bytes 18874884 | tf_op jit(solution)/shard_map/dot_general | solution.py:74
  (72 shorter events, 13.4 us)
Async XLA Ops:
  7.2 51.1 %all-reduce.2.cloned.1.call-start = ((), (), s32[]{:S(2)}) async-start(), calls=%async_computation.2 | async-start | bytes 1048576 | tf_op jit(solution)/shard_map/psum | solution.py:64
  8.3 5.5 %copy-start.1 = (bf16[512,2048]{1,0:T(8,128)(2,1)S(1)}, bf16[512,2048]{1,0:T(8,128)(2,1)}, u32[]{:S(2)}) copy-start(bf16[512,2048]{1,0:T(8,128)(2,1)} %param.8) | copy-start | bytes 6291460
  8.3 5.5 %copy-start.7 = (bf16[2048,1024]{1,0:T(8,128)(2,1)S(1)}, bf16[2048,1024]{1,0:T(8,128)(2,1)}, u32[]{:S(2)}) copy-start(bf16[2048,1024]{1,0:T(8,128)(2,1)} %param.11) | copy-start | bytes 12582916
  13.8 3.4 copy-start.5
  13.8 3.4 copy-start.6
  17.1 84.9 %all-gather.7.cloned.1.call-start = ((), (), s32[]{:S(2)}) async-start(), calls=%async_computation.4 | async-start | bytes 1310720 | tf_op jit(solution)/shard_map/all_gather | solution.py:78
  59.3 4.7 copy-start.2
  61.8 76.8 %all-gather.9.cloned.1.call-start = ((), (), s32[]{:S(2)}) async-start(), calls=%async_computation.5 | async-start | bytes 10485760 | tf_op jit(solution)/shard_map/all_gather | solution.py:76
  62.6 135.8 %all-gather.11.cloned.1.call-start = ((), (), s32[]{:S(2)}) async-start(), calls=%async_computation.6 | async-start | bytes 10485760 | tf_op jit(solution)/shard_map/all_gather | solution.py:77
  63.2 286.3 %all-gather.5.cloned.1.call-start = ((), (), s32[]{:S(2)}) async-start(), calls=%async_computation.1 | async-start | bytes 10485760 | tf_op jit(solution)/shard_map/all_gather | solution.py:67
  63.8 430.6 %reduce-scatter.2.cloned.1.call-start = ((), (), s32[]{:S(2)}) async-start(), calls=%async_computation.3 | async-start | bytes 10485760 | tf_op jit(solution)/shard_map/reduce_scatter | solution.py:72
  88.4 0.7 copy-start.4
  89.5 7.7 %copy-start.3 = (bf16[512,1024]{1,0:T(8,128)(2,1)S(1)}, bf16[512,1024]{1,0:T(8,128)(2,1)}, u32[]{:S(2)}) copy-start(bf16[512,1024]{1,0:T(8,128)(2,1)} %get-tuple-element.17) | copy-start | bytes 3145732
  89.5 8.0 %copy-start.8 = (bf16[1024,2048]{1,0:T(8,128)(2,1)S(1)}, bf16[1024,2048]{1,0:T(8,128)(2,1)}, u32[]{:S(2)}) copy-start(bf16[1024,2048]{1,0:T(8,128)(2,1)} %param.12) | copy-start | bytes 12582916
  102.0 7.8 %copy-start = (bf16[2048,256]{1,0:T(8,128)(2,1)S(1)}, bf16[2048,256]{1,0:T(8,128)(2,1)}, u32[]{:S(2)}) copy-start(bf16[2048,256]{1,0:T(8,128)(2,1)} %all-gather.7.cloned.1.call-done) | copy-start | bytes 3145732
Sparse Core Ops, SparseCore 0:
  17.2 40.9 all-reduce.1
  62.0 16.6 all-gather.6
  80.3 58.2 all-gather.8
  140.0 58.2 all-gather.10
  199.8 149.6 all-gather.4
  351.6 142.6 reduce-scatter.1
where the time goes:
time: 512 us; the launch traced here: 511 us
  waiting for transfers between devices  354 us (69%)
  matrix products  109 us (21%)
  local copies, waits for them, and re-layouts  27.7 us (5%)
  between operations  14.4 us (3%)
  other arithmetic  6.18 us (1%)
    all_gather x1, waiting for transfers between devices, local(): all_inputs = lax.all_gather(inputs, 'tensor', axis=1, tiled=True)  136 us
    reduce_scatter x1, waiting for transfers between devices, local(): lax.psum_scatter(others, 'tensor', scatter_dimension=1, tiled=True)  120 us
    psum x1, waiting for transfers between devices, local(): folded = lax.psum(folded, 'tensor')  40.7 us
    all_gather x1, waiting for transfers between devices, local(): group_cotangent = lax.all_gather(cotangent, 'dp', axis=0, tiled=True)  35.6 us
    unnamed x45, local copies, waits for them, and re-layouts  25.8 us
    dot_general x1, matrix products, local(): jnp.dot(all_inputs, weight, preferred_element_type=jnp.float32)  24.9 us
    dot_general x1, matrix products, local(): lax.dot_general(cotangent, weight, TRAILING, preferred_element_type=jnp.f...  24.4 us
    all_gather x1, waiting for transfers between devices, local(): group_inputs = lax.all_gather(inputs, 'dp', axis=0, tiled=True)  19.4 us
  transfers between devices with their start and end apart: 6, of which 5 were waited for; matrix products, arithmetic and copies ran while one was open for 23% of the time, Pallas kernels for 0%

commit v1 on v0

--- a/solution.py
+++ b/solution.py
@@ -64,7 +64,23 @@
     folded = lax.psum(folded, "tensor")
     scaled_down_f = (coef_folded * folded[:, :LANES]).astype(jnp.bfloat16)
     scaled_back_f = (coef_folded * folded[:, LANES:]).astype(jnp.bfloat16)
-    all_inputs = lax.all_gather(inputs, "tensor", axis=1, tiled=True)
+    ways, here, hop = (lax.axis_size("tensor"), lax.axis_index("tensor"), inputs.shape[1])
+    lengths = [n * ways if d == 1 else n for d, n in enumerate(inputs.shape)]
+    full = lax.dynamic_update_slice_in_dim(
+        jnp.zeros(lengths, inputs.dtype), inputs, here * hop, axis=1
+    )
+    going_up = going_down = inputs
+    for far in range(1, ways // 2 + 1):
+        going_up = lax.ppermute(going_up, "tensor", [(d, (d + 1) % ways) for d in range(ways)])
+        full = lax.dynamic_update_slice_in_dim(full, going_up, (here - far) % ways * hop, axis=1)
+        if 2 * far < ways:
+            going_down = lax.ppermute(
+                going_down, "tensor", [(d, (d - 1) % ways) for d in range(ways)]
+            )
+            full = lax.dynamic_update_slice_in_dim(
+                full, going_down, (here + far) % ways * hop, axis=1
+            )
+    all_inputs = full
     mine = lax.axis_index("tensor")
     block = jnp.arange(weight.shape[0], dtype=jnp.int32) // feature_local
     frozen_back = lax.dot_general(cotangent, weight, TRAILING, preferred_element_type=jnp.float32)

time: 512 us -> 363 us (0.71)
  waiting for transfers between devices: 354 us -> 187 us
  local copies, waits for them, and re-layouts: 27.7 us -> 39.3 us
    all_gather x1 -> x0, waiting for transfers between devices: 136 us -> none  [local(): all_inputs = lax.all_gather(inputs, 'tensor', axis=1, tiled=True)]
    ppermute x0 -> x3, waiting for transfers between devices: none -> 70.3 us  [the longest x2 38.7 us: local(): lax.ppermute(going_up, 'tensor', [(d, (d + 1) % ways) for d in range(ways)])]
    reduce_scatter x1, waiting for transfers between devices: 120 us -> 75.9 us  [local(): lax.psum_scatter(others, 'tensor', scatter_dimension=1, tiled=True)]
    all_gather x1, waiting for transfers between devices: 35.6 us -> 0.01 us  [local(): group_cotangent = lax.all_gather(cotangent, 'dp', axis=0, tiled=True)]
    all_gather x1, waiting for transfers between devices: 19.4 us -> 0.01 us  [local(): group_inputs = lax.all_gather(inputs, 'dp', axis=0, tiled=True)]
    dynamic_update_slice x0 -> x4, local copies, waits for them, and re-layouts: none -> 11.1 us  [the longest x2 6.32 us: local(): lax.dynamic_update_slice_in_dim(full, going_up, (here - far) % ways * hop...]
    unnamed x45 -> x51, local copies, waits for them, and re-layouts: 25.8 us -> 22.7 us
  transfers between devices with their start and end apart: 6 -> 8, of which waited for: 5 -> 4; matrix products, arithmetic and copies ran while one was open for 23% -> 36% of each run, Pallas kernels for 0% -> 0%
where the time goes in v1:
time: 363 us; the launch traced here: 362 us
  waiting for transfers between devices  187 us (52%)
  matrix products  110 us (30%)
  local copies, waits for them, and re-layouts  39.3 us (11%)
  between operations  14.2 us (4%)
  other arithmetic  8.02 us (2%)
  starting transfers between devices  4.08 us (1%)
    reduce_scatter x1, waiting for transfers between devices, local(): lax.psum_scatter(others, 'tensor', scatter_dimension=1, tiled=True)  75.9 us
    psum x1, waiting for transfers between devices, local(): folded = lax.psum(folded, 'tensor')  39.4 us
    ppermute x2, waiting for transfers between devices, local(): lax.ppermute(going_up, 'tensor', [(d, (d + 1) % ways) for d in range(ways)])  38.7 us
    ppermute x1, waiting for transfers between devices, local(): lax.ppermute(going_down, 'tensor', [(d, (d - 1) % ways) for d in range(wa...  31.5 us
    dot_general x1, matrix products, local(): jnp.dot(all_inputs, weight, preferred_element_type=jnp.float32)  25.4 us
    dot_general x1, matrix products, local(): lax.dot_general(cotangent, weight, TRAILING, preferred_element_type=jnp.f...  25.2 us
    unnamed x51, local copies, waits for them, and re-layouts  22.7 us
    dot_general x1, matrix products, local(): lax.dot_general(down_all, group_cotangent, FIRST, preferred_element_type=...  15 us
  transfers between devices with their start and end apart: 8, of which 4 were waited for; matrix products, arithmetic and copies ran while one was open for 36% of the time, Pallas kernels for 0%

profile of v1, /device:TPU:0, one launch (start us, length us, event | category | flops | bytes accessed | tf_op | source)
XLA Modules:
  0.0 362.4 jit_solution(2097231501993026895)
XLA Ops:
  8.3 5.3 %compare_select_fusion.4 = f32[512,1024]{1,0:T(8,128)S(1)} fusion(bf16[512,2048]{1,0:T(8,128)(2,1)} %param.9, bf16[1024,2048]{1,0:T(8,128)(2,1)} %param.12, s32[1024]{0:T(1024)S(1)} %add_select_fusion.1, s32[512]{0:T(512)S(1)} %select_reduce_fusion.3), kind=kOutput, calls=%fused_computation.9 | convolution fusion | flops 2148532224 | bytes 8394752 | tf_op jit(solution)/shard_map/dot_general | solution.py:58
  13.8 2.3 compare_select_fusion.5
  17.3 1.6 compare_select_fusion.6
  18.9 39.4 %all-reduce.2.cloned.1.call-done = f32[512,256]{1,0:T(8,128)} async-done(((f32[512,256]{1,0:T(8,128)}), f32[512,256]{1,0:T(8,128)}) %all-reduce.2.cloned.1.call-update) | async-done | bytes 524304 | tf_op jit(solution)/shard_map/psum | solution.py:64
  58.2 1.7 constant_dynamic-update-slice_fusion.15
  60.0 1.6 constant_dynamic-update-slice_fusion.7
  65.0 2.6 collective-permute-start.1
  67.6 25.2 %select_convert_fusion = bf16[512,8192]{1,0:T(8,128)(2,1)} fusion(bf16[512,2048]{1,0:T(8,128)(2,1)} %param.9, bf16[8192,2048]{1,0:T(8,128)(2,1)} %param.10, pred[8192]{0:T(1024)(128)(4,1)S(1)} %fusion.23), kind=kOutput, calls=%fused_computation | convolution fusion | flops 17188257792 | bytes 44048384 | tf_op jit(solution)/shard_map/dot_general | solution.py:86
  93.7 4.4 %broadcast_in_dim.130 = bf16[512,8192]{1,0:T(8,128)(2,1)} broadcast(bf16[]{:T(256)} %constant.82.clone.1), dimensions={} | broadcast | bytes 8388610 | tf_op jit(solution)/shard_map/broadcast_in_dim | solution.py:70
  98.1 1.6 constant_dynamic-update-slice_fusion.19
  104.7 7.1 %fusion.13 = f32[512,2048]{1,0:T(8,128)} fusion(bf16[1024,2048]{1,0:T(8,128)(2,1)} %param.12, bf16[512,1024]{1,0:T(8,128)(2,1)} %constant_dynamic-update-slice_fusion, s32[1024]{0:T(1024)S(1)} %add_select_fusion.1, s32[512]{0:T(512)S(1)} %select_reduce_fusion.3), kind=kOutput, calls=%fused_computation.24 | convolution fusion | flops 2148532224 | bytes 9443328 | tf_op jit(solution)/shard_map/dot_general | solution.py:100
  111.7 4.4 %fusion.14 = f32[512,2048]{1,0:T(8,128)} fusion(bf16[2048,1024]{1,0:T(8,128)(2,1)S(1)} %copy-done.10, bf16[512,1024]{1,0:T(8,128)(2,1)S(1)} %constant_dynamic-update-slice_fusion.8, s32[1024]{0:T(1024)S(1)} %add_select_fusion.1, s32[512]{0:T(512)S(1)} %select_reduce_fusion.3), kind=kOutput, calls=%fused_computation.25 | convolution fusion | flops 2148532224 | bytes 9443328 | tf_op jit(solution)/shard_map/dot_general | solution.py:104
  121.7 3.2 constant_dynamic-update-slice_fusion.18
  125.8 31.5 %collective-permute-done.1 = bf16[512,2048]{1,0:T(8,128)(2,1)} collective-permute-done((bf16[512,2048]{1,0:T(8,128)(2,1)S(1)}, bf16[512,2048]{1,0:T(8,128)(2,1)}, u32[]{:S(2)}, u32[]{:S(2)}) %collective-permute-start.1) | collective-permute-done | bytes 2097184 | tf_op jit(solution)/shard_map/ppermute | solution.py:77
  157.3 3.2 constant_dynamic-update-slice_fusion.17
  161.2 2.1 copy-done.5
  163.3 38.7 %collective-permute-done.2 = bf16[512,2048]{1,0:T(8,128)(2,1)} collective-permute-done((bf16[512,2048]{1,0:T(8,128)(2,1)}, bf16[512,2048]{1,0:T(8,128)(2,1)}, u32[]{:S(2)}, u32[]{:S(2)}) %collective-permute-start.2) | collective-permute-done | bytes 2097184 | tf_op jit(solution)/shard_map/ppermute | solution.py:74
  202.0 3.2 constant_dynamic-update-slice_fusion.16
  205.2 25.4 %select_convert_fusion.1 = bf16[512,2048]{1,0:T(8,128)(2,1)} fusion(f32[512,2048]{1,0:T(8,128)S(1)} %copy-done.11, bf16[512,8192]{1,0:T(8,128)(2,1)} %constant_dynamic-update-slice_fusion.16, bf16[8192,2048]{1,0:T(8,128)(2,1)} %param.10, pred[512]{0:T(512)(128)(4,1)S(1)} %broadcast_compare_fusion), kind=kOutput, calls=%fused_computation.19 | convolution fusion | flops 17183014912 | bytes 48235008 | tf_op jit(solution)/shard_map/dot_general | solution.py:97
  230.5 14.9 %multiply_bitcast_fusion.1 = f32[1,2048,1024]{1,2,0:T(8,128)} fusion(bf16[2048,2048]{1,0:T(8,128)(2,1)} %all-gather.6.cloned.1.call-done, bf16[2048,1024]{1,0:T(8,128)(2,1)} %copy-done.5, f32[1024]{0:T(1024)S(1)} %compare_select_fusion.12, s32[1024]{0:T(1024)S(1)} %add_select_fusion.1, s32[2048]{0:T(1024)S(1)} %bitcast.30), kind=kOutput, calls=%fused_computation.4 | convolution fusion | flops 8596226048 | bytes 20987904 | tf_op jit(solution)/shard_map/dot_general | solution.py:111
  245.4 9.2 %copy.15 = f32[1,2048,1024]{2,1,0:T(8,128)} copy(f32[1,2048,1024]{1,2,0:T(8,128)} %multiply_bitcast_fusion.1) | data formatting | bytes 16777216
  254.6 15.0 %multiply_bitcast_fusion = f32[1,1024,2048]{2,1,0:T(8,128)} fusion(bf16[2048,2048]{1,0:T(8,128)(2,1)} %all-gather.8.cloned.1.call-done, bf16[2048,1024]{1,0:T(8,128)(2,1)} %copy-done.4, f32[1024]{0:T(1024)S(1)} %compare_select_fusion.12, s32[1024]{0:T(1024)S(1)} %add_select_fusion.1, s32[2048]{0:T(1024)S(1)} %bitcast.31), kind=kOutput, calls=%fused_computation.3 | convolution fusion | flops 8596226048 | bytes 20987904 | tf_op jit(solution)/shard_map/dot_general | solution.py:112
  269.7 75.9 %reduce-scatter.2.cloned.1.call-done = bf16[512,2048]{1,0:T(8,128)(2,1)} async-done(((bf16[512,8192]{1,0:T(8,128)(2,1)}), bf16[512,2048]{1,0:T(8,128)(2,1)}) %reduce-scatter.2.cloned.1.call-update) | async-done | bytes 2097168 | tf_op jit(solution)/shard_map/reduce_scatter | solution.py:88
  345.6 10.3 %fusion.4 = bf16[512,2048]{1,0:T(8,128)(2,1)} fusion(f32[512,2048]{1,0:T(8,128)} %fusion.14, bf16[512,2048]{1,0:T(8,128)(2,1)} %reduce-scatter.2.cloned.1.call-done, bf16[512,2048]{1,0:T(8,128)(2,1)S(1)} %copy-done.3, bf16[8192,2048]{1,0:T(8,128)(2,1)} %param.10, s32[]{:T(128)S(6)} %select_n.142, pred[512]{0:T(512)(128)(4,1)S(1)} %broadcast_compare_fusion), kind=kOutput, calls=%fused_computation.16 | convolution fusion | flops 4300210176 | bytes 18874884 | tf_op jit(solution)/shard_map/dot_general | solution.py:90
  (86 shorter events, 18.4 us)
Async XLA Ops:
  7.2 51.1 %all-reduce.2.cloned.1.call-start = ((), (), s32[]{:S(2)}) async-start(), calls=%async_computation.1 | async-start | bytes 1048576 | tf_op jit(solution)/shard_map/psum | solution.py:64
  8.3 5.5 %copy-start.1 = (bf16[512,2048]{1,0:T(8,128)(2,1)S(1)}, bf16[512,2048]{1,0:T(8,128)(2,1)}, u32[]{:S(2)}) copy-start(bf16[512,2048]{1,0:T(8,128)(2,1)} %param.8) | copy-start | bytes 6291460
  8.3 5.5 %copy-start.9 = (bf16[2048,1024]{1,0:T(8,128)(2,1)S(1)}, bf16[2048,1024]{1,0:T(8,128)(2,1)}, u32[]{:S(2)}) copy-start(bf16[2048,1024]{1,0:T(8,128)(2,1)} %param.11) | copy-start | bytes 12582916
  13.8 3.4 copy-start.7
  13.8 3.4 copy-start.8
  17.1 99.1 %all-gather.4.cloned.1.call-start = ((), (), s32[]{:S(2)}) async-start(), calls=%async_computation.3 | async-start | bytes 1310720 | tf_op jit(solution)/shard_map/all_gather | solution.py:94
  18.9 44.9 %copy-start.2 = (bf16[512,2048]{1,0:T(8,128)(2,1)S(1)}, bf16[512,2048]{1,0:T(8,128)(2,1)}, u32[]{:S(2)}) copy-start(bf16[512,2048]{1,0:T(8,128)(2,1)} %param.8) | copy-start | bytes 6291460
  62.4 168.2 %all-gather.6.cloned.1.call-start = ((), (), s32[]{:S(2)}) async-start(), calls=%async_computation.4 | async-start | bytes 10485760 | tf_op jit(solution)/shard_map/all_gather | solution.py:92
  63.1 191.6 %all-gather.8.cloned.1.call-start = ((), (), s32[]{:S(2)}) async-start(), calls=%async_computation.5 | async-start | bytes 10485760 | tf_op jit(solution)/shard_map/all_gather | solution.py:93
  63.7 281.9 %reduce-scatter.2.cloned.1.call-start = ((), (), s32[]{:S(2)}) async-start(), calls=%async_computation.2 | async-start | bytes 10485760 | tf_op jit(solution)/shard_map/reduce_scatter | solution.py:88
  63.7 52.4 %collective-permute-start = (bf16[512,2048]{1,0:T(8,128)(2,1)S(1)}, bf16[512,2048]{1,0:T(8,128)(2,1)}, u32[]{:S(2)}, u32[]{:S(2)}) collective-permute-start(bf16[512,2048]{1,0:T(8,128)(2,1)S(1)} %copy-done.2), channel_id=1, source_target_pairs={{0,4},{4,8},{8,12},{12,0},{1,5},{5,9},{9,13},{13,1},{2,6},{6,10},{... | collective-permute-start | bytes 6291464 | tf_op jit(solution)/shard_map/ppermute | solution.py:74
  65.0 92.3 %collective-permute-start.1 = (bf16[512,2048]{1,0:T(8,128)(2,1)S(1)}, bf16[512,2048]{1,0:T(8,128)(2,1)}, u32[]{:S(2)}, u32[]{:S(2)}) collective-permute-start(bf16[512,2048]{1,0:T(8,128)(2,1)S(1)} %copy-done.2), channel_id=1, source_target_pairs={{0,12},{4,0},{8,4},{12,8},{1,13},{5,1},{9,5},{13,9},{2,14},{6,2},{... | collective-permute-start | bytes 6291464 | tf_op jit(solution)/shard_map/ppermute | solution.py:77
  92.9 0.7 copy-start.6
  104.6 7.1 %copy-start.10 = (bf16[2048,1024]{1,0:T(8,128)(2,1)S(1)}, bf16[2048,1024]{1,0:T(8,128)(2,1)}, u32[]{:S(2)}) copy-start(bf16[2048,1024]{1,0:T(8,128)(2,1)} %param.11) | copy-start | bytes 12582916
  116.2 85.8 %collective-permute-start.2 = (bf16[512,2048]{1,0:T(8,128)(2,1)}, bf16[512,2048]{1,0:T(8,128)(2,1)}, u32[]{:S(2)}, u32[]{:S(2)}) collective-permute-start(bf16[512,2048]{1,0:T(8,128)(2,1)} %collective-permute-done), channel_id=1, source_target_pairs={{0,4},{4,8},{8,12},{12,0},{1,5},{5,9},{9,13},{13,1},{2,6},{6,10},{... | collective-permute-start | bytes 6291464 | tf_op jit(solution)/shard_map/ppermute | solution.py:74
  116.2 5.0 %copy-start = (bf16[2048,256]{1,0:T(8,128)(2,1)S(1)}, bf16[2048,256]{1,0:T(8,128)(2,1)}, u32[]{:S(2)}) copy-start(bf16[2048,256]{1,0:T(8,128)(2,1)} %all-gather.4.cloned.1.call-done) | copy-start | bytes 3145732
  125.2 35.5 %copy-start.4 = (bf16[2048,1024]{1,0:T(8,128)(2,1)}, bf16[2048,1024]{1,0:T(8,128)(2,1)S(1)}, u32[]{:S(2)}) copy-start(bf16[2048,1024]{1,0:T(8,128)(2,1)S(1)} %get-tuple-element.19) | copy-start | bytes 12582916
  160.5 44.7 %copy-start.11 = (f32[512,2048]{1,0:T(8,128)S(1)}, f32[512,2048]{1,0:T(8,128)}, u32[]{:S(2)}) copy-start(f32[512,2048]{1,0:T(8,128)} %fusion.13) | copy-start | bytes 12582916
  161.2 2.1 copy-start.5
  254.6 90.9 %copy-start.3 = (bf16[512,2048]{1,0:T(8,128)(2,1)S(1)}, bf16[512,2048]{1,0:T(8,128)(2,1)}, u32[]{:S(2)}) copy-start(bf16[512,2048]{1,0:T(8,128)(2,1)} %param.9) | copy-start | bytes 6291460
Sparse Core Ops, SparseCore 0:
  17.2 40.9 all-reduce.1
  62.5 16.6 all-gather.3
  80.8 58.2 all-gather.5
  140.5 58.2 all-gather.7
  201.0 144.4 reduce-scatter.1
